TPU v7x, 32 devices: a whole 2x2x4 slice. The times are simulated.
32 devices in a mesh: lon: 4 (over y, core), lat: 4 (over z), dp: 2 (over x).
Axes of the slice: x: 2, y: 2, z: 4, core: 2. Of those that a mesh axis runs over, the one named last changes fastest.
Arguments:
- tokens: bfloat16 [2, 2, 24, 48, 192], P('dp', None, 'lat', 'lon'), may hold values from -6 to 6
- grad_out: bfloat16 [2, 2, 24, 48, 192], P('dp', None, 'lat', 'lon'), may hold values from -6 to 6
- qkv_weight: bfloat16 [576, 192], P('dp'), may hold values from -0.4375 to 0.4375
- proj_weight: bfloat16 [192, 192], P('dp'), may hold values from -0.4375 to 0.4375
- norm_gain: bfloat16 [192], P('dp'), may hold values from 0.5 to 1.5
- bias_table: float32 [4, 6, 3312], P('lat'), may hold values from -2.5 to 402.5
Outputs:
- grad_tokens: bfloat16 [2, 2, 24, 48, 192], P('dp', None, 'lat', 'lon')
- grad_qkv_weight: float32 [576, 192], P('dp')
- grad_proj_weight: float32 [192, 192], P('dp')
- grad_norm_gain: float32 [192], P('dp')
- grad_bias_table: float32 [4, 6, 3312], P('lat')
All inputs are finite; a program needn't handle non-finite values.
Results may differ from a plain program's by a relative error of at most 0.015.
Values may be sent and summed in bfloat16 or wider, within the bound.
No kernel may reach another device: no remote copies, remote signals or barrier semaphores. Data moves between devices by JAX's collectives and lax.ppermute only.
A program may use at most 64 MiB of HBM per device.

v0:
```python
import math
import jax
import jax.numpy as jnp
from jax import lax
from jax.sharding import PartitionSpec as P

C = 192
H = 6
HD = 32
WZ = 2
WA = 6
WL = 12
SA = 3
SO = 6
WT = 144
POS = 3312
EPS = 1e-05
MASKED = -1e30


def passed_along(value, axis, steps):
    count = lax.axis_size(axis)
    pairs = [(source, (source + steps) % count) for source in range(count)]
    return lax.ppermute(value, axis, pairs)


def shortened(shard):
    return jax.tree.map(lambda a: a.astype(jnp.bfloat16) if a.dtype == jnp.float32 else a, shard)


def offsets_table():
    first = jnp.arange(WL)[:, None, None]
    second = jnp.arange(WL)[None, :, None]
    offset = jnp.arange(2 * WL - 1)[None, None, :]
    return (offset == first - second + WL - 1).astype(jnp.float32)


def spread_bias(table, onehot):
    window_rows = WZ * WA
    shaped = table.reshape(table.shape[0], H, window_rows, window_rows, 2 * WL - 1)
    spread = jnp.einsum("ghabr,uvr->ghaubv", shaped, onehot, precision=lax.Precision.HIGHEST)
    return spread.reshape(table.shape[0], H, WT, WT)


def gather_bias(grad_full, onehot):
    window_rows = WZ * WA
    shaped = grad_full.reshape(grad_full.shape[0], H, window_rows, WL, window_rows, WL)
    folded = jnp.einsum("ghaubv,uvr->ghabr", shaped, onehot, precision=lax.Precision.HIGHEST)
    return folded.reshape(grad_full.shape[0], H, POS)


def to_windows(grid, lat_rows, lon_cols):
    members, levels, channels = (grid.shape[0], grid.shape[1], grid.shape[4])
    lat_types = lat_rows // WA
    lon_windows = lon_cols // WL
    parts = grid.reshape(members, levels, lat_types, WA, lon_windows, WL, channels)
    parts = parts.transpose(2, 0, 4, 1, 3, 5, 6)
    return parts.reshape(lat_types, members * lon_windows, WT, channels)


def from_windows(blocks, members, lat_rows, lon_cols):
    lat_types = lat_rows // WA
    lon_windows = lon_cols // WL
    channels = blocks.shape[-1]
    parts = blocks.reshape(lat_types, members, lon_windows, WZ, WA, WL, channels)
    return parts.transpose(1, 3, 0, 4, 2, 5, 6).reshape(members, WZ, lat_rows, lon_cols, channels)


def window_grads(
    window_x, window_dy, window_flag, table, qkv_weight, proj_weight, norm_gain, onehot
):
    groups, count = (window_x.shape[0], window_x.shape[1])
    flat_x = window_x.reshape(-1, C).astype(jnp.float32)
    average = jnp.mean(flat_x, axis=-1, keepdims=True)
    centred = flat_x - average
    variance = jnp.mean(centred * centred, axis=-1, keepdims=True)
    inverse = lax.rsqrt(variance + EPS)
    unit = centred * inverse
    gain_value = norm_gain.astype(jnp.float32)
    normed = (unit * gain_value).astype(jnp.bfloat16)
    projected = jnp.dot(normed, qkv_weight.T, preferred_element_type=jnp.float32).astype(
        jnp.bfloat16
    )
    split = projected.reshape(groups, count, WT, 3, H, HD)
    queries = split[:, :, :, 0]
    key_part = split[:, :, :, 1]
    values = split[:, :, :, 2]
    head_scale = 1.0 / math.sqrt(HD)
    bias_full = spread_bias(table, onehot)
    scores = (
        jnp.einsum("gwqhd,gwkhd->gwhqk", queries, key_part, preferred_element_type=jnp.float32)
        * head_scale
    )
    scores = scores + bias_full[:, None]
    allowed = window_flag[:, :, None, :, None] == window_flag[:, :, None, None, :]
    scores = jnp.where(allowed, scores, MASKED)
    highest = jnp.max(scores, axis=-1, keepdims=True)
    expo = jnp.exp(scores - highest)
    probs = expo / jnp.sum(expo, axis=-1, keepdims=True)
    probs_low = probs.astype(jnp.bfloat16)
    attended = jnp.einsum(
        "gwhqk,gwkhd->gwqhd", probs_low, values, preferred_element_type=jnp.float32
    )
    attended = attended.astype(jnp.bfloat16).reshape(-1, C)
    flat_dy = window_dy.reshape(-1, C)
    grad_proj = jnp.dot(flat_dy.T, attended, preferred_element_type=jnp.float32)
    grad_att = jnp.dot(flat_dy, proj_weight, preferred_element_type=jnp.float32).astype(
        jnp.bfloat16
    )
    grad_att = grad_att.reshape(groups, count, WT, H, HD)
    grad_probs = jnp.einsum(
        "gwqhd,gwkhd->gwhqk", grad_att, values, preferred_element_type=jnp.float32
    )
    grad_values = jnp.einsum(
        "gwhqk,gwqhd->gwkhd", probs_low, grad_att, preferred_element_type=jnp.float32
    )
    grad_scores = probs * (grad_probs - jnp.sum(probs * grad_probs, axis=-1, keepdims=True))
    scores_low = grad_scores.astype(jnp.bfloat16)
    grad_queries = (
        jnp.einsum("gwhqk,gwkhd->gwqhd", scores_low, key_part, preferred_element_type=jnp.float32)
        * head_scale
    )
    grad_keys = (
        jnp.einsum("gwhqk,gwqhd->gwkhd", scores_low, queries, preferred_element_type=jnp.float32)
        * head_scale
    )
    grad_qkv = (
        jnp.stack([grad_queries, grad_keys, grad_values], axis=3)
        .reshape(-1, 3 * C)
        .astype(jnp.bfloat16)
    )
    grad_qkv_w = jnp.dot(grad_qkv.T, normed, preferred_element_type=jnp.float32)
    grad_normed = jnp.dot(grad_qkv, qkv_weight, preferred_element_type=jnp.float32)
    grad_gain = jnp.sum(grad_normed * unit, axis=0)
    scaled = grad_normed * gain_value
    grad_x = inverse * (
        scaled
        - jnp.mean(scaled, axis=-1, keepdims=True)
        - unit * jnp.mean(scaled * unit, axis=-1, keepdims=True)
    )
    grad_table = gather_bias(jnp.sum(grad_scores, axis=1), onehot)
    return (grad_x.reshape(groups, count, WT, C), grad_qkv_w, grad_proj, grad_gain, grad_table)


def body(tokens, grad_out, qkv_weight, proj_weight, norm_gain, bias_table):
    full_qkv, full_proj, full_gain = (
        lax.all_gather(qkv_weight, "dp", axis=0, tiled=True),
        lax.all_gather(proj_weight, "dp", axis=0, tiled=True),
        lax.all_gather(norm_gain, "dp", axis=0, tiled=True),
    )
    members, levels, lat_rows, lon_cols = (
        tokens.shape[0],
        tokens.shape[1],
        tokens.shape[2],
        tokens.shape[3],
    )
    ahead = passed_along((tokens[:, :, :, :SO], grad_out[:, :, :, :SO]), "lon", -1)
    lon_tokens = jnp.concatenate([tokens[:, :, :, SO:], ahead[0]], axis=3)
    lon_grads = jnp.concatenate([grad_out[:, :, :, SO:], ahead[1]], axis=3)
    above = passed_along((lon_tokens[:, :, :SA], lon_grads[:, :, :SA]), "lat", -1)
    shifted = jnp.concatenate([lon_tokens[:, :, SA:], above[0]], axis=2)
    shifted_dy = jnp.concatenate([lon_grads[:, :, SA:], above[1]], axis=2)
    pole_device = lax.axis_index("lat") == lax.axis_size("lat") - 1
    wrapped = jnp.logical_and(jnp.arange(lat_rows) >= lat_rows - SA, pole_device)
    grid_shape = (members, levels, lat_rows, lon_cols, 1)
    flag_grid = jnp.broadcast_to(wrapped[None, None, :, None, None], grid_shape)
    outputs = window_grads(
        to_windows(shifted, lat_rows, lon_cols),
        to_windows(shifted_dy, lat_rows, lon_cols),
        to_windows(flag_grid, lat_rows, lon_cols)[..., 0],
        bias_table,
        full_qkv,
        full_proj,
        full_gain,
        offsets_table(),
    )
    grad_blocks, grad_qkv_w, grad_proj, grad_gain, grad_table = outputs
    table_sum = lax.psum(grad_table, ("lon", "dp"))
    grad_shifted = from_windows(grad_blocks, members, lat_rows, lon_cols)
    below = passed_along(grad_shifted[:, :, lat_rows - SA :].astype(jnp.bfloat16), "lat", 1).astype(
        jnp.float32
    )
    lat_restored = jnp.concatenate([below, grad_shifted[:, :, : lat_rows - SA]], axis=2)
    behind = passed_along(shortened(lat_restored[:, :, :, lon_cols - SO :]), "lon", 1)
    restored = jnp.concatenate([behind, lat_restored[:, :, :, : lon_cols - SO]], axis=3)
    grad_tokens = (grad_out.astype(jnp.float32) + restored).astype(jnp.bfloat16)
    summed = lax.psum((grad_qkv_w, grad_proj, grad_gain), ("lon", "lat"))
    shares = (
        lax.psum_scatter(
            summed[0].astype(jnp.bfloat16), "dp", scatter_dimension=0, tiled=True
        ).astype(jnp.float32),
        lax.psum_scatter(
            summed[1].astype(jnp.bfloat16), "dp", scatter_dimension=0, tiled=True
        ).astype(jnp.float32),
        lax.psum_scatter(
            summed[2].astype(jnp.bfloat16), "dp", scatter_dimension=0, tiled=True
        ).astype(jnp.float32),
    )
    return (grad_tokens, shares[0], shares[1], shares[2], table_sum)


def solution(mesh):
    return jax.shard_map(
        body,
        mesh=mesh,
        in_specs=(
            P("dp", None, "lat", "lon", None),
            P("dp", None, "lat", "lon", None),
            P("dp", None),
            P("dp", None),
            P("dp"),
            P("lat", None, None),
        ),
        out_specs=(
            P("dp", None, "lat", "lon", None),
            P("dp", None),
            P("dp", None),
            P("dp"),
            P("lat", None, None),
        ),
        check_vma=False,
    )
```

profile of v0, /device:TPU:0, one launch (start us, length us, event | category | flops | bytes accessed | tf_op | source)
XLA Modules:
  0.0 192.5 jit_solution(13003009651287583203)
XLA Ops:
  8.1 0.9 fusion.26
  9.0 2.5 %collective-permute-start = (bf16[1,2,6,6,192]{4,1,3,2,0:T(2,128)(2,1)S(1)}, bf16[1,2,6,6,192]{4,1,3,2,0:T(2,128)(2,1)S(1)}, u32[]{:S(2)}, u32[]{:S(2)}) collective-permute-start(bf16[1,2,6,6,192]{4,1,3,2,0:T(2,128)(2,1)S(1)} %get-tuple-element.24), channel_id=1, source_target_pairs={{0,24},{8,0},{16,8},{24,16},{1,25},{9,1},{17,9},{25,17},{2,26},{10... | collective-permute-start | bytes 82952 | tf_op jit(solution)/shard_map/ppermute | solution.py:24
  11.4 0.8 fusion.27
  12.3 0.7 collective-permute-start.2
  13.0 1.1 reduce.8
  14.8 4.9 %convolution_bitcast_fusion = f32[1,6,12,12,12,12]{4,5,2,1,3,0:T(8,128)} fusion(f32[6,12,12,23,1]{3,2,1,0,4:T(8,128)S(1)} %reshape.415, pred[12,12,23,1,1]{2,0,1,4,3:T(8,128)(4,1)S(1)} %fusion.16), kind=kOutput, calls=%fused_computation.1 | convolution fusion | flops 34338816 | bytes 580464 | tf_op jit(solution)/shard_map/ghabr,uvr->ghaubv/dot_general | solution.py:41
  19.7 6.3 %all_gather.10 = bf16[576,192]{1,0:T(8,128)(2,1)S(1)} all-gather(bf16[288,192]{1,0:T(8,128)(2,1)S(1)} %copy-done.5), channel_id=1, replica_groups=mesh['lon'=4,'lat'=4,'dp'=2] {'dp'}, dimensions={0}, use_global_device_ids=true | all-gather | bytes 331776 | tf_op jit(solution)/shard_map/all_gather | solution.py:147
  27.4 4.9 %all-reduce = bf16[192]{0:T(256)(128)(2,1)S(1)} all-reduce(bf16[192]{0:T(256)(128)(2,1)S(1)} %dynamic-update-slice), channel_id=1, replica_groups=mesh['lon'=4,'lat'=4,'dp'=2] {'dp'}, use_global_device_ids=true, to_apply=%add | all-reduce | flops 192 | bytes 768
  32.4 11.7 %copy.70 = f32[1,6,12,12,12,12]{3,2,5,4,1,0:T(8,128)} copy(f32[1,6,12,12,12,12]{4,5,2,1,3,0:T(8,128)} %convolution_bitcast_fusion) | data formatting | bytes 995328 | tf_op jit(solution)/shard_map/broadcast_in_dim;reshape | solution.py:94
  44.1 4.9 %reshape.419 = f32[6,144,144]{1,2,0:T(8,128)S(1)} reshape(f32[1,6,12,12,12,12]{3,2,5,4,1,0:T(8,128)} %copy.70) | data formatting | bytes 995328 | tf_op jit(solution)/shard_map/broadcast_in_dim;reshape | solution.py:94
  49.0 4.8 %all_gather.11 = bf16[192,192]{1,0:T(8,128)(2,1)S(1)} all-gather(bf16[96,192]{1,0:T(8,128)(2,1)S(1)} %copy-done.9), channel_id=1, replica_groups=mesh['lon'=4,'lat'=4,'dp'=2] {'dp'}, dimensions={0}, use_global_device_ids=true | all-gather | bytes 110592 | tf_op jit(solution)/shard_map/all_gather | solution.py:148
  53.9 3.7 %collective-permute-start.1 = (bf16[1,2,3,12,192]{4,1,3,2,0:T(2,128)(2,1)S(1)}, bf16[1,2,3,12,192]{4,1,3,2,0:T(2,128)(2,1)S(1)}, u32[]{:S(2)}, u32[]{:S(2)}) collective-permute-start(bf16[1,2,3,12,192]{4,1,3,2,0:T(2,128)(2,1)S(1)} %get-tuple-element.22), channel_id=1, source_target_pairs={{0,6},{2,0},{4,2},{6,4},{1,7},{3,1},{5,3},{7,5},{8,14},{10,8},{12,... | collective-permute-start | bytes 82952 | tf_op jit(solution)/shard_map/ppermute | solution.py:24
  57.7 0.7 collective-permute-start.3
  58.4 0.8 collective-permute-done.1
  60.4 1.5 collective-permute-done.3
  62.2 0.8 copy.52
  63.8 0.8 fusion.29
  64.6 1.9 convolution_bitcast_fusion.2
  66.5 1.2 multiply_reduce_fusion
  67.7 0.8 subtract_multiply_fusion
  69.0 1.0 convolution_convert_fusion.1
  70.1 5.0 %reshape.406 = f32[6,12,12,12,12]{2,1,4,3,0:T(8,128)} reshape(f32[6,144,144]{1,2,0:T(8,128)S(1)} %subtract_multiply_fusion) | data formatting | bytes 995328 | tf_op jit(solution)/shard_map/reshape.46
  76.3 6.0 %convolution_bitcast_fusion.1 = f32[6,12,12,23]{3,1,2,0:T(8,128)S(1)} fusion(f32[6,12,12,12,12]{2,1,4,3,0:T(8,128)} %reshape.406, s32[12,12]{0,1:T(8,128)S(1)} %copy-done.8), kind=kOutput, calls=%fused_computation.7 | convolution fusion | flops 34342128 | bytes 577728 | tf_op jit(solution)/shard_map/ghaubv,uvr->ghabr/dot_general | solution.py:48
  82.5 0.9 reshape.407
  83.4 77.7 %all-reduce.7 = (bf16[576,192]{1,0:T(8,128)(2,1)}, bf16[192,192]{1,0:T(8,128)(2,1)}, bf16[192]{0:T(256)(128)(2,1)S(1)}) all-reduce(f32[576,192]{1,0:T(8,128)S(1)} %fusion.30, f32[192,192]{1,0:T(8,128)S(1)} %fusion.31, f32[192]{0:T(256)S(1)} %get-tuple-element.15), channel_id=1, replica_groups=mesh['lon'=4,'lat'=4,'dp'=2] {'lon','lat'}, use_global_device_ids=true, to_apply=%region_7.8 | all-reduce | flops 147648 | bytes 885888 | tf_op jit(solution)/shard_map/psum | solution.py:187
  162.2 4.9 %all-reduce.1 = bf16[192]{0:T(256)(128)(2,1)S(1)} all-reduce(bf16[192]{0:T(256)(128)(2,1)S(1)} %get-tuple-element.20), channel_id=4, replica_groups=mesh['lon'=4,'lat'=4,'dp'=2] {'dp'}, use_global_device_ids=true, to_apply=%region_13.14.clone | all-reduce | flops 192 | bytes 768
  168.1 1.6 copy.60
  169.7 1.3 collective-permute-done.5
  171.1 0.7 copy.59
  171.8 1.4 convert_element_type.150
  173.2 10.2 %reduce-scatter.3.cloned.1.call-done = bf16[288,192]{1,0:T(8,128)(2,1)} async-done(((bf16[576,192]{1,0:T(8,128)(2,1)}), bf16[288,192]{1,0:T(8,128)(2,1)}) %reduce-scatter.3.cloned.1.call-update) | async-done | bytes 110608 | tf_op jit(solution)/shard_map/reduce_scatter | solution.py:189
  183.4 1.6 convert_element_type.145
  (98 shorter events, 7.1 us)
Async XLA Ops:
  8.0 17.9 %copy-start.15 = (u32[32]{0:T(128)S(1)}, u32[32]{0:T(128)}, u32[]{:S(2)}) copy-start(u32[32]{0:T(128)} %constant.36) | copy-start | bytes 388
  8.0 11.7 %copy-start.5 = (bf16[288,192]{1,0:T(8,128)(2,1)S(1)}, bf16[288,192]{1,0:T(8,128)(2,1)}, u32[]{:S(2)}) copy-start(bf16[288,192]{1,0:T(8,128)(2,1)} %param.8) | copy-start | bytes 331780
  8.0 19.2 %copy-start.16 = (bf16[96]{0:T(256)(128)(2,1)S(1)}, bf16[96]{0:T(256)(128)(2,1)}, u32[]{:S(2)}) copy-start(bf16[96]{0:T(256)(128)(2,1)} %param.10) | copy-start | bytes 580
  8.0 160.1 %all-reduce.6.cloned.1.call-start = ((), (), s32[]{:S(2)}) async-start(), calls=%async_computation.4 | async-start | bytes 212992 | tf_op jit(solution)/shard_map/psum | solution.py:178
  9.0 44.9 %collective-permute-start = (bf16[1,2,6,6,192]{4,1,3,2,0:T(2,128)(2,1)S(1)}, bf16[1,2,6,6,192]{4,1,3,2,0:T(2,128)(2,1)S(1)}, u32[]{:S(2)}, u32[]{:S(2)}) collective-permute-start(bf16[1,2,6,6,192]{4,1,3,2,0:T(2,128)(2,1)S(1)} %get-tuple-element.24), channel_id=1, source_target_pairs={{0,24},{8,0},{16,8},{24,16},{1,25},{9,1},{17,9},{25,17},{2,26},{10... | collective-permute-start | bytes 82952 | tf_op jit(solution)/shard_map/ppermute | solution.py:24
  12.3 45.3 %collective-permute-start.2 = (bf16[1,2,6,6,192]{4,1,3,2,0:T(2,128)(2,1)S(1)}, bf16[1,2,6,6,192]{4,1,3,2,0:T(2,128)(2,1)S(1)}, u32[]{:S(2)}, u32[]{:S(2)}) collective-permute-start(bf16[1,2,6,6,192]{4,1,3,2,0:T(2,128)(2,1)S(1)} %get-tuple-element.28), channel_id=1, source_target_pairs={{0,24},{8,0},{16,8},{24,16},{1,25},{9,1},{17,9},{25,17},{2,26},{10... | collective-permute-start | bytes 82952 | tf_op jit(solution)/shard_map/ppermute | solution.py:24
  13.0 19.4 %copy-start.7 = (s32[12,12]{0,1:T(8,128)}, s32[12,12]{0,1:T(8,128)S(1)}, u32[]{:S(2)}) copy-start(s32[12,12]{0,1:T(8,128)S(1)} %subtract_add_fusion) | copy-start | bytes 1732
  44.1 5.0 %copy-start.9 = (bf16[96,192]{1,0:T(8,128)(2,1)S(1)}, bf16[96,192]{1,0:T(8,128)(2,1)}, u32[]{:S(2)}) copy-start(bf16[96,192]{1,0:T(8,128)(2,1)} %param.9) | copy-start | bytes 110596
  53.9 5.3 %collective-permute-start.1 = (bf16[1,2,3,12,192]{4,1,3,2,0:T(2,128)(2,1)S(1)}, bf16[1,2,3,12,192]{4,1,3,2,0:T(2,128)(2,1)S(1)}, u32[]{:S(2)}, u32[]{:S(2)}) collective-permute-start(bf16[1,2,3,12,192]{4,1,3,2,0:T(2,128)(2,1)S(1)} %get-tuple-element.22), channel_id=1, source_target_pairs={{0,6},{2,0},{4,2},{6,4},{1,7},{3,1},{5,3},{7,5},{8,14},{10,8},{12,... | collective-permute-start | bytes 82952 | tf_op jit(solution)/shard_map/ppermute | solution.py:24
  57.7 4.2 %collective-permute-start.3 = (bf16[1,2,3,12,192]{4,1,3,2,0:T(2,128)(2,1)S(1)}, bf16[1,2,3,12,192]{4,1,3,2,0:T(2,128)(2,1)S(1)}, u32[]{:S(2)}, u32[]{:S(2)}) collective-permute-start(bf16[1,2,3,12,192]{4,1,3,2,0:T(2,128)(2,1)S(1)} %get-tuple-element.26), channel_id=1, source_target_pairs={{0,6},{2,0},{4,2},{6,4},{1,7},{3,1},{5,3},{7,5},{8,14},{10,8},{12,... | collective-permute-start | bytes 82952 | tf_op jit(solution)/shard_map/ppermute | solution.py:24
  59.2 0.6 copy-start
  59.7 3.7 %copy-start.2 = (f32[2,6,12]{0,2,1:T(8,128)}, f32[2,6,12]{0,2,1:T(8,128)S(1)}, u32[]{:S(2)}) copy-start(f32[2,6,12]{0,2,1:T(8,128)S(1)} %add_rsqrt_fusion) | copy-start | bytes 1732
  60.1 3.3 %copy-start.11 = (f32[144]{0:T(256)}, f32[144]{0:T(256)S(1)}, u32[]{:S(2)}) copy-start(f32[144]{0:T(256)S(1)} %div.25) | copy-start | bytes 1732
  60.3 3.1 %copy-start.13 = (f32[144]{0:T(256)}, f32[144]{0:T(256)S(1)}, u32[]{:S(2)}) copy-start(f32[144]{0:T(256)S(1)} %rsqrt.13) | copy-start | bytes 1732
  64.6 3.1 %copy-start.10 = (f32[6,144]{1,0:T(8,128)}, f32[6,144]{1,0:T(8,128)S(1)}, u32[]{:S(2)}) copy-start(f32[6,144]{1,0:T(8,128)S(1)} %get-tuple-element.31) | copy-start | bytes 10372
  68.5 6.5 %copy-start.6 = (bf16[1,1,144,1,6,32]{2,5,4,3,1,0:T(8,128)(2,1)S(1)}, bf16[1,1,144,1,6,32]{2,5,4,3,1,0:T(8,128)(2,1)}, u32[]{:S(2)}) copy-start(bf16[1,1,144,1,6,32]{2,5,4,3,1,0:T(8,128)(2,1)} %convolution_bitcast_fusion.2) | copy-start | bytes 165892
  68.5 6.6 %copy-start.12 = (f32[144]{0:T(256)S(1)}, f32[144]{0:T(256)}, u32[]{:S(2)}) copy-start(f32[144]{0:T(256)} %copy-done.11) | copy-start | bytes 1732
  68.5 6.6 %copy-start.14 = (f32[144]{0:T(256)S(1)}, f32[144]{0:T(256)}, u32[]{:S(2)}) copy-start(f32[144]{0:T(256)} %copy-done.13) | copy-start | bytes 1732
  68.8 6.8 %copy-start.1 = (bf16[1,2,3,12,192]{4,1,3,2,0:T(2,128)(2,1)S(1)}, bf16[1,2,3,12,192]{4,1,3,2,0:T(2,128)(2,1)}, u32[]{:S(2)}) copy-start(bf16[1,2,3,12,192]{4,1,3,2,0:T(2,128)(2,1)} %copy-done) | copy-start | bytes 82948
  68.8 6.7 %copy-start.3 = (f32[2,6,12]{0,2,1:T(8,128)S(1)}, f32[2,6,12]{0,2,1:T(8,128)}, u32[]{:S(2)}) copy-start(f32[2,6,12]{0,2,1:T(8,128)} %copy-done.2) | copy-start | bytes 1732
  69.0 7.3 %copy-start.8 = (s32[12,12]{0,1:T(8,128)S(1)}, s32[12,12]{0,1:T(8,128)}, u32[]{:S(2)}) copy-start(s32[12,12]{0,1:T(8,128)} %copy-done.7) | copy-start | bytes 1732
  75.8 95.2 %copy-start.4 = (bf16[1,2,6,12,192]{4,1,3,2,0:T(2,128)(2,1)S(1)}, bf16[1,2,6,12,192]{4,1,3,2,0:T(2,128)(2,1)}, u32[]{:S(2)}) copy-start(bf16[1,2,6,12,192]{4,1,3,2,0:T(2,128)(2,1)} %param.7) | copy-start | bytes 165892
  83.4 88.4 %reduce-scatter.5.cloned.1.call-start = ((), (), s32[]{:S(2)}) async-start(), calls=%async_computation.3 | async-start | bytes 147456 | tf_op jit(solution)/shard_map/reduce_scatter | solution.py:192
  161.2 22.2 %reduce-scatter.3.cloned.1.call-start = ((), (), s32[]{:S(2)}) async-start(), calls=%async_computation.2 | async-start | bytes 442368 | tf_op jit(solution)/shard_map/reduce_scatter | solution.py:189
  161.5 5.9 %collective-permute-start.4 = (bf16[1,2,3,12,192]{4,3,2,1,0:T(8,128)(2,1)S(1)}, bf16[1,2,3,12,192]{4,3,2,1,0:T(8,128)(2,1)S(1)}, u32[]{:S(2)}, u32[]{:S(2)}) collective-permute-start(bf16[1,2,3,12,192]{4,3,2,1,0:T(8,128)(2,1)S(1)} %slice.103), channel_id=1, source_target_pairs={{0,2},{2,4},{4,6},{6,0},{1,3},{3,5},{5,7},{7,1},{8,10},{10,12},{12... | collective-permute-start | bytes 82952 | tf_op jit(solution)/shard_map/ppermute | solution.py:24
  167.4 3.6 %collective-permute-start.5 = (bf16[1,2,6,6,192]{4,3,2,1,0:T(8,128)(2,1)S(1)}, bf16[1,2,6,6,192]{4,3,2,1,0:T(8,128)(2,1)S(1)}, u32[]{:S(2)}, u32[]{:S(2)}) collective-permute-start(bf16[1,2,6,6,192]{4,3,2,1,0:T(8,128)(2,1)S(1)} %fusion.15), channel_id=1, source_target_pairs={{0,8},{8,16},{16,24},{24,0},{1,9},{9,17},{17,25},{25,1},{2,10},{10... | collective-permute-start | bytes 82952 | tf_op jit(solution)/shard_map/ppermute | solution.py:24
Sparse Core Ops, SparseCore 0:
  83.5 51.0 all-reduce.5
Sparse Core Ops, SparseCore 1:
  161.3 7.5 reduce-scatter.4
  171.5 11.9 reduce-scatter.2
where the time goes:
time: 193 us
  blocking collectives  98.6 us (51%)
  local copies, waits for them, and re-layouts  29.6 us (15%)
  between operations  17.3 us (9%)
  matrix products  17 us (9%)
  waiting for transfers between devices  14.2 us (7%)
  other arithmetic  8 us (4%)
  starting transfers between devices  7.77 us (4%)
    psum x1, blocking collectives, body(): summed = lax.psum((grad_qkv_w, grad_proj, grad_gain), ('lon', 'lat'))  77.7 us
    another operation x2, local copies, waits for them, and re-layouts, window_grads(): scores = scores + bias_full[:, None]  16.6 us
    reduce_scatter x1, waiting for transfers between devices, body(): lax.psum_scatter(summed[0].astype(jnp.bfloat16), 'dp', scatter_dimension=...  10.2 us
    unnamed x2, blocking collectives  9.86 us
    ppermute x6, starting transfers between devices, passed_along(): return lax.ppermute(value, axis, pairs)  7.64 us
    all_gather x1, blocking collectives, body(): lax.all_gather(qkv_weight, 'dp', axis=0, tiled=True)  6.26 us
    dot_general x1, matrix products, gather_bias(): jnp.einsum('ghaubv,uvr->ghabr', shaped, onehot, precision=lax.Precision.H...  5.99 us
    another operation x2, local copies, waits for them, and re-layouts  5.3 us
  transfers between devices with their start and end apart: 9, of which 5 were waited for; matrix products, arithmetic and copies ran while one was open for 16% of the time, Pallas kernels for 0%

commit v1 on v0

--- a/solution.py
+++ b/solution.py
@@ -184,7 +184,9 @@
     behind = passed_along(shortened(lat_restored[:, :, :, lon_cols - SO :]), "lon", 1)
     restored = jnp.concatenate([behind, lat_restored[:, :, :, : lon_cols - SO]], axis=3)
     grad_tokens = (grad_out.astype(jnp.float32) + restored).astype(jnp.bfloat16)
-    summed = lax.psum((grad_qkv_w, grad_proj, grad_gain), ("lon", "lat"))
+    summed = jax.lax.psum(
+        jax.lax.psum((grad_qkv_w, grad_proj, grad_gain), axis_name="lat"), axis_name="lon"
+    )
     shares = (
         lax.psum_scatter(
             summed[0].astype(jnp.bfloat16), "dp", scatter_dimension=0, tiled=True

time: 193 us -> 221 us (1.15)
  waiting for transfers between devices: 14.2 us -> 86.1 us
  blocking collectives: 98.6 us -> 53.6 us
    psum x1 -> x2, blocking collectives: 77.7 us -> 32.5 us  [the longest x1 21.4 us: body(): jax.lax.psum(jax.lax.psum((grad_qkv_w, grad_proj, grad_gain), axis_name='...]
    psum x0 -> x1, waiting for transfers between devices: none -> 34 us  [body(): jax.lax.psum((grad_qkv_w, grad_proj, grad_gain), axis_name='lat')]
    psum x1, waiting for transfers between devices: 0.01 us -> 25.6 us  [body(): table_sum = lax.psum(grad_table, ('lon', 'dp'))]
    reduce_scatter x1, waiting for transfers between devices: 0.01 us -> 5.61 us  [body(): lax.psum_scatter(summed[1].astype(jnp.bfloat16), 'dp', scatter_dimension=...]
    ppermute x6, waiting for transfers between devices: 3.91 us -> 7.45 us  [passed_along(): return lax.ppermute(value, axis, pairs)]
    reduce_scatter x1, waiting for transfers between devices: 10.2 us -> 13.4 us  [body(): lax.psum_scatter(summed[0].astype(jnp.bfloat16), 'dp', scatter_dimension=...]
  transfers between devices with their start and end apart: 9 -> 10, of which waited for: 5 -> 7; matrix products, arithmetic and copies ran while one was open for 16% -> 17% of each run, Pallas kernels for 0% -> 0%
where the time goes in v1:
time: 221 us; the launch traced here: 220 us
  waiting for transfers between devices  86.1 us (39%)
  blocking collectives  53.6 us (24%)
  local copies, waits for them, and re-layouts  29.6 us (13%)
  matrix products  18.6 us (8%)
  between operations  15.6 us (7%)
  starting transfers between devices  8.61 us (4%)
  other arithmetic  8 us (4%)
    psum x1, waiting for transfers between devices, body(): jax.lax.psum((grad_qkv_w, grad_proj, grad_gain), axis_name='lat')  34 us
    psum x1, waiting for transfers between devices, body(): table_sum = lax.psum(grad_table, ('lon', 'dp'))  25.6 us
    psum x1, blocking collectives, body(): jax.lax.psum(jax.lax.psum((grad_qkv_w, grad_proj, grad_gain), axis_name='...  21.4 us
    another operation x2, local copies, waits for them, and re-layouts, window_grads(): scores = scores + bias_full[:, None]  16.6 us
    reduce_scatter x1, waiting for transfers between devices, body(): lax.psum_scatter(summed[0].astype(jnp.bfloat16), 'dp', scatter_dimension=...  13.4 us
    psum x1, blocking collectives, body(): jax.lax.psum((grad_qkv_w, grad_proj, grad_gain), axis_name='lat')  11.1 us
    unnamed x2, blocking collectives  10 us
    ppermute x6, starting transfers between devices, passed_along(): return lax.ppermute(value, axis, pairs)  8.26 us
  transfers between devices with their start and end apart: 10, of which 7 were waited for; matrix products, arithmetic and copies ran while one was open for 17% of the time, Pallas kernels for 0%

profile of v1, /device:TPU:0, one launch (start us, length us, event | category | flops | bytes accessed | tf_op | source)
XLA Modules:
  0.0 220.1 jit_solution(9611155773095604916)
XLA Ops:
  7.2 0.9 fusion.26
  8.1 2.5 %collective-permute-start = (bf16[1,2,6,6,192]{4,1,3,2,0:T(2,128)(2,1)S(1)}, bf16[1,2,6,6,192]{4,1,3,2,0:T(2,128)(2,1)S(1)}, u32[]{:S(2)}, u32[]{:S(2)}) collective-permute-start(bf16[1,2,6,6,192]{4,1,3,2,0:T(2,128)(2,1)S(1)} %get-tuple-element.26), channel_id=1, source_target_pairs={{0,24},{8,0},{16,8},{24,16},{1,25},{9,1},{17,9},{25,17},{2,26},{10... | collective-permute-start | bytes 82952 | tf_op jit(solution)/shard_map/ppermute | solution.py:24
  12.2 1.1 reduce.8
  14.0 4.9 %convolution_bitcast_fusion = f32[1,6,12,12,12,12]{4,5,2,1,3,0:T(8,128)} fusion(f32[6,12,12,23,1]{3,2,1,0,4:T(8,128)S(1)} %reshape.415, pred[12,12,23,1,1]{2,0,1,4,3:T(8,128)(4,1)S(1)} %fusion.16), kind=kOutput, calls=%fused_computation.1 | convolution fusion | flops 34338816 | bytes 580464 | tf_op jit(solution)/shard_map/ghabr,uvr->ghaubv/dot_general | solution.py:41
  18.9 6.3 %all_gather.10 = bf16[576,192]{1,0:T(8,128)(2,1)S(1)} all-gather(bf16[288,192]{1,0:T(8,128)(2,1)S(1)} %copy-done.5), channel_id=1, replica_groups=mesh['lon'=4,'lat'=4,'dp'=2] {'dp'}, dimensions={0}, use_global_device_ids=true | all-gather | bytes 331776 | tf_op jit(solution)/shard_map/all_gather | solution.py:147
  26.6 4.9 %all-reduce = bf16[192]{0:T(256)(128)(2,1)S(1)} all-reduce(bf16[192]{0:T(256)(128)(2,1)S(1)} %dynamic-update-slice), channel_id=1, replica_groups=mesh['lon'=4,'lat'=4,'dp'=2] {'dp'}, use_global_device_ids=true, to_apply=%add | all-reduce | flops 192 | bytes 768
  31.5 11.7 %copy.70 = f32[1,6,12,12,12,12]{3,2,5,4,1,0:T(8,128)} copy(f32[1,6,12,12,12,12]{4,5,2,1,3,0:T(8,128)} %convolution_bitcast_fusion) | data formatting | bytes 995328 | tf_op jit(solution)/shard_map/broadcast_in_dim;reshape | solution.py:94
  43.3 4.9 %reshape.419 = f32[6,144,144]{1,2,0:T(8,128)S(1)} reshape(f32[1,6,12,12,12,12]{3,2,5,4,1,0:T(8,128)} %copy.70) | data formatting | bytes 995328 | tf_op jit(solution)/shard_map/broadcast_in_dim;reshape | solution.py:94
  48.2 4.8 %all_gather.11 = bf16[192,192]{1,0:T(8,128)(2,1)S(1)} all-gather(bf16[96,192]{1,0:T(8,128)(2,1)S(1)} %copy-done.9), channel_id=1, replica_groups=mesh['lon'=4,'lat'=4,'dp'=2] {'dp'}, dimensions={0}, use_global_device_ids=true | all-gather | bytes 110592 | tf_op jit(solution)/shard_map/all_gather | solution.py:148
  53.1 3.7 %collective-permute-start.1 = (bf16[1,2,3,12,192]{4,1,3,2,0:T(2,128)(2,1)S(1)}, bf16[1,2,3,12,192]{4,1,3,2,0:T(2,128)(2,1)S(1)}, u32[]{:S(2)}, u32[]{:S(2)}) collective-permute-start(bf16[1,2,3,12,192]{4,1,3,2,0:T(2,128)(2,1)S(1)} %get-tuple-element.24), channel_id=1, source_target_pairs={{0,6},{2,0},{4,2},{6,4},{1,7},{3,1},{5,3},{7,5},{8,14},{10,8},{12,... | collective-permute-start | bytes 82952 | tf_op jit(solution)/shard_map/ppermute | solution.py:24
  57.4 1.0 collective-permute-done.1
  59.5 1.4 collective-permute-done.3
  63.6 1.9 convolution_bitcast_fusion.2
  65.4 1.2 multiply_reduce_fusion
  68.0 1.0 convolution_convert_fusion.1
  69.0 5.0 %reshape.406 = f32[6,12,12,12,12]{2,1,4,3,0:T(8,128)} reshape(f32[6,144,144]{1,2,0:T(8,128)S(1)} %subtract_multiply_fusion) | data formatting | bytes 995328 | tf_op jit(solution)/shard_map/reshape.46
  74.8 1.0 fusion.30
  75.9 0.9 fusion.31
  76.8 11.1 %psum.53 = f32[192]{0:T(256)S(1)} all-reduce(f32[192]{0:T(256)S(1)} %get-tuple-element.15), channel_id=1, replica_groups=mesh['lon'=4,'lat'=4,'dp'=2] {'lat'}, use_global_device_ids=true, to_apply=%region_14.15 | all-reduce | flops 192 | bytes 1536 | tf_op jit(solution)/shard_map/psum | solution.py:188
  88.2 6.1 %convolution_bitcast_fusion.1 = f32[6,12,12,23]{3,1,2,0:T(8,128)S(1)} fusion(f32[6,12,12,12,12]{2,1,4,3,0:T(8,128)} %reshape.406, s32[12,12]{0,1:T(8,128)S(1)} %copy-done.8), kind=kOutput, calls=%fused_computation.7 | convolution fusion | flops 34342128 | bytes 577728 | tf_op jit(solution)/shard_map/ghaubv,uvr->ghabr/dot_general | solution.py:48
  94.4 0.9 reshape.407
  95.4 34.0 %all-reduce.10.cloned.1.call-done = (f32[576,192]{1,0:T(8,128)}, f32[192,192]{1,0:T(8,128)}) async-done(((f32[576,192]{1,0:T(8,128)}, f32[192,192]{1,0:T(8,128)}), (f32[576,192]{1,0:T(8,128)}, f32[192,192]{1,0:T(8,128)})) %all-reduce.10.cloned.1.call-update) | async-done | bytes 589840 | tf_op jit(solution)/shard_map/psum | solution.py:188
  129.4 21.4 %all-reduce.11 = (bf16[576,192]{1,0:T(8,128)(2,1)}, bf16[192,192]{1,0:T(8,128)(2,1)}, bf16[192]{0:T(256)(128)(2,1)S(1)}) all-reduce(f32[576,192]{1,0:T(8,128)} %get-tuple-element.18, f32[192,192]{1,0:T(8,128)} %get-tuple-element.19, f32[192]{0:T(256)S(1)} %psum.53), channel_id=1, replica_groups=mesh['lon'=4,'lat'=4,'dp'=2] {'lon'}, use_global_device_ids=true, to_apply=%region_8.9 | all-reduce | flops 147648 | bytes 885888 | tf_op jit(solution)/shard_map/psum | solution.py:187
  151.1 0.9 collective-permute-start.4
  152.0 5.1 %collective-permute-done.4 = bf16[1,2,3,12,192]{4,3,2,1,0:T(8,128)(2,1)S(1)} collective-permute-done((bf16[1,2,3,12,192]{4,3,2,1,0:T(8,128)(2,1)S(1)}, bf16[1,2,3,12,192]{4,3,2,1,0:T(8,128)(2,1)S(1)}, u32[]{:S(2)}, u32[]{:S(2)}) %collective-permute-start.4) | collective-permute-done | bytes 27680 | tf_op jit(solution)/shard_map/ppermute | solution.py:24
  157.8 25.6 %all-reduce.8.cloned.1.call-done = f32[1,6,3312]{2,1,0:T(8,128)} async-done(((f32[1,6,3312]{2,1,0:T(8,128)}), f32[1,6,3312]{2,1,0:T(8,128)}) %all-reduce.8.cloned.1.call-update) | async-done | bytes 79504 | tf_op jit(solution)/shard_map/psum | solution.py:178
  183.4 1.6 copy.60
  185.8 5.1 %all-reduce.1 = bf16[192]{0:T(256)(128)(2,1)S(1)} all-reduce(bf16[192]{0:T(256)(128)(2,1)S(1)} %get-tuple-element.22), channel_id=4, replica_groups=mesh['lon'=4,'lat'=4,'dp'=2] {'dp'}, use_global_device_ids=true, to_apply=%region_16.17.clone | all-reduce | flops 192 | bytes 768
  191.5 5.6 %reduce-scatter.5.cloned.1.call-done = bf16[96,192]{1,0:T(8,128)(2,1)} async-done(((bf16[192,192]{1,0:T(8,128)(2,1)}), bf16[96,192]{1,0:T(8,128)(2,1)}) %reduce-scatter.5.cloned.1.call-update) | async-done | bytes 36880 | tf_op jit(solution)/shard_map/reduce_scatter | solution.py:194
  197.1 1.4 convert_element_type.150
  198.6 13.4 %reduce-scatter.3.cloned.1.call-done = bf16[288,192]{1,0:T(8,128)(2,1)} async-done(((bf16[576,192]{1,0:T(8,128)(2,1)}), bf16[288,192]{1,0:T(8,128)(2,1)}) %reduce-scatter.3.cloned.1.call-update) | async-done | bytes 110608 | tf_op jit(solution)/shard_map/reduce_scatter | solution.py:191
  211.9 1.6 convert_element_type.145
  (102 shorter events, 11.7 us)
Async XLA Ops:
  7.2 17.9 %copy-start.15 = (u32[32]{0:T(128)S(1)}, u32[32]{0:T(128)}, u32[]{:S(2)}) copy-start(u32[32]{0:T(128)} %constant.36) | copy-start | bytes 388
  7.2 11.7 %copy-start.5 = (bf16[288,192]{1,0:T(8,128)(2,1)S(1)}, bf16[288,192]{1,0:T(8,128)(2,1)}, u32[]{:S(2)}) copy-start(bf16[288,192]{1,0:T(8,128)(2,1)} %param.8) | copy-start | bytes 331780
  7.2 19.2 %copy-start.16 = (bf16[96]{0:T(256)(128)(2,1)S(1)}, bf16[96]{0:T(256)(128)(2,1)}, u32[]{:S(2)}) copy-start(bf16[96]{0:T(256)(128)(2,1)} %param.10) | copy-start | bytes 580
  7.2 122.2 %all-reduce.10.cloned.1.call-start = ((), (), s32[]{:S(2)}) async-start(), calls=%async_computation.5 | async-start | bytes 1572864 | tf_op jit(solution)/shard_map/psum | solution.py:188
  8.1 44.9 %collective-permute-start = (bf16[1,2,6,6,192]{4,1,3,2,0:T(2,128)(2,1)S(1)}, bf16[1,2,6,6,192]{4,1,3,2,0:T(2,128)(2,1)S(1)}, u32[]{:S(2)}, u32[]{:S(2)}) collective-permute-start(bf16[1,2,6,6,192]{4,1,3,2,0:T(2,128)(2,1)S(1)} %get-tuple-element.26), channel_id=1, source_target_pairs={{0,24},{8,0},{16,8},{24,16},{1,25},{9,1},{17,9},{25,17},{2,26},{10... | collective-permute-start | bytes 82952 | tf_op jit(solution)/shard_map/ppermute | solution.py:24
  11.4 45.3 %collective-permute-start.2 = (bf16[1,2,6,6,192]{4,1,3,2,0:T(2,128)(2,1)S(1)}, bf16[1,2,6,6,192]{4,1,3,2,0:T(2,128)(2,1)S(1)}, u32[]{:S(2)}, u32[]{:S(2)}) collective-permute-start(bf16[1,2,6,6,192]{4,1,3,2,0:T(2,128)(2,1)S(1)} %get-tuple-element.30), channel_id=1, source_target_pairs={{0,24},{8,0},{16,8},{24,16},{1,25},{9,1},{17,9},{25,17},{2,26},{10... | collective-permute-start | bytes 82952 | tf_op jit(solution)/shard_map/ppermute | solution.py:24
  12.2 19.4 %copy-start.7 = (s32[12,12]{0,1:T(8,128)}, s32[12,12]{0,1:T(8,128)S(1)}, u32[]{:S(2)}) copy-start(s32[12,12]{0,1:T(8,128)S(1)} %subtract_add_fusion) | copy-start | bytes 1732
  43.2 5.0 %copy-start.9 = (bf16[96,192]{1,0:T(8,128)(2,1)S(1)}, bf16[96,192]{1,0:T(8,128)(2,1)}, u32[]{:S(2)}) copy-start(bf16[96,192]{1,0:T(8,128)(2,1)} %param.9) | copy-start | bytes 110596
  53.1 5.3 %collective-permute-start.1 = (bf16[1,2,3,12,192]{4,1,3,2,0:T(2,128)(2,1)S(1)}, bf16[1,2,3,12,192]{4,1,3,2,0:T(2,128)(2,1)S(1)}, u32[]{:S(2)}, u32[]{:S(2)}) collective-permute-start(bf16[1,2,3,12,192]{4,1,3,2,0:T(2,128)(2,1)S(1)} %get-tuple-element.24), channel_id=1, source_target_pairs={{0,6},{2,0},{4,2},{6,4},{1,7},{3,1},{5,3},{7,5},{8,14},{10,8},{12,... | collective-permute-start | bytes 82952 | tf_op jit(solution)/shard_map/ppermute | solution.py:24
  56.9 4.0 %collective-permute-start.3 = (bf16[1,2,3,12,192]{4,1,3,2,0:T(2,128)(2,1)S(1)}, bf16[1,2,3,12,192]{4,1,3,2,0:T(2,128)(2,1)S(1)}, u32[]{:S(2)}, u32[]{:S(2)}) collective-permute-start(bf16[1,2,3,12,192]{4,1,3,2,0:T(2,128)(2,1)S(1)} %get-tuple-element.28), channel_id=1, source_target_pairs={{0,6},{2,0},{4,2},{6,4},{1,7},{3,1},{5,3},{7,5},{8,14},{10,8},{12,... | collective-permute-start | bytes 82952 | tf_op jit(solution)/shard_map/ppermute | solution.py:24
  58.4 0.6 copy-start
  58.9 3.5 %copy-start.2 = (f32[2,6,12]{0,2,1:T(8,128)}, f32[2,6,12]{0,2,1:T(8,128)S(1)}, u32[]{:S(2)}) copy-start(f32[2,6,12]{0,2,1:T(8,128)S(1)} %add_rsqrt_fusion) | copy-start | bytes 1732
  59.3 3.1 %copy-start.11 = (f32[144]{0:T(256)}, f32[144]{0:T(256)S(1)}, u32[]{:S(2)}) copy-start(f32[144]{0:T(256)S(1)} %div.25) | copy-start | bytes 1732
  59.5 2.9 %copy-start.13 = (f32[144]{0:T(256)}, f32[144]{0:T(256)S(1)}, u32[]{:S(2)}) copy-start(f32[144]{0:T(256)S(1)} %rsqrt.13) | copy-start | bytes 1732
  63.6 3.1 %copy-start.10 = (f32[6,144]{1,0:T(8,128)}, f32[6,144]{1,0:T(8,128)S(1)}, u32[]{:S(2)}) copy-start(f32[6,144]{1,0:T(8,128)S(1)} %get-tuple-element.33) | copy-start | bytes 10372
  67.5 6.5 %copy-start.6 = (bf16[1,1,144,1,6,32]{2,5,4,3,1,0:T(8,128)(2,1)S(1)}, bf16[1,1,144,1,6,32]{2,5,4,3,1,0:T(8,128)(2,1)}, u32[]{:S(2)}) copy-start(bf16[1,1,144,1,6,32]{2,5,4,3,1,0:T(8,128)(2,1)} %convolution_bitcast_fusion.2) | copy-start | bytes 165892
  67.5 6.6 %copy-start.12 = (f32[144]{0:T(256)S(1)}, f32[144]{0:T(256)}, u32[]{:S(2)}) copy-start(f32[144]{0:T(256)} %copy-done.11) | copy-start | bytes 1732
  67.5 6.6 %copy-start.14 = (f32[144]{0:T(256)S(1)}, f32[144]{0:T(256)}, u32[]{:S(2)}) copy-start(f32[144]{0:T(256)} %copy-done.13) | copy-start | bytes 1732
  67.8 6.8 %copy-start.1 = (bf16[1,2,3,12,192]{4,1,3,2,0:T(2,128)(2,1)S(1)}, bf16[1,2,3,12,192]{4,1,3,2,0:T(2,128)(2,1)}, u32[]{:S(2)}) copy-start(bf16[1,2,3,12,192]{4,1,3,2,0:T(2,128)(2,1)} %copy-done) | copy-start | bytes 82948
  67.8 6.7 %copy-start.3 = (f32[2,6,12]{0,2,1:T(8,128)S(1)}, f32[2,6,12]{0,2,1:T(8,128)}, u32[]{:S(2)}) copy-start(f32[2,6,12]{0,2,1:T(8,128)} %copy-done.2) | copy-start | bytes 1732
  68.0 20.2 %copy-start.8 = (s32[12,12]{0,1:T(8,128)S(1)}, s32[12,12]{0,1:T(8,128)}, u32[]{:S(2)}) copy-start(s32[12,12]{0,1:T(8,128)} %copy-done.7) | copy-start | bytes 1732
  75.9 109.2 %copy-start.4 = (bf16[1,2,6,12,192]{4,1,3,2,0:T(2,128)(2,1)S(1)}, bf16[1,2,6,12,192]{4,1,3,2,0:T(2,128)(2,1)}, u32[]{:S(2)}) copy-start(bf16[1,2,6,12,192]{4,1,3,2,0:T(2,128)(2,1)} %param.7) | copy-start | bytes 165892
  87.9 95.5 %all-reduce.8.cloned.1.call-start = ((), (), s32[]{:S(2)}) async-start(), calls=%async_computation.4 | async-start | bytes 212992 | tf_op jit(solution)/shard_map/psum | solution.py:178
  95.3 101.8 %reduce-scatter.5.cloned.1.call-start = ((), (), s32[]{:S(2)}) async-start(), calls=%async_computation.3 | async-start | bytes 147456 | tf_op jit(solution)/shard_map/reduce_scatter | solution.py:194
  150.9 61.1 %reduce-scatter.3.cloned.1.call-start = ((), (), s32[]{:S(2)}) async-start(), calls=%async_computation.2 | async-start | bytes 442368 | tf_op jit(solution)/shard_map/reduce_scatter | solution.py:191
  151.1 5.9 %collective-permute-start.4 = (bf16[1,2,3,12,192]{4,3,2,1,0:T(8,128)(2,1)S(1)}, bf16[1,2,3,12,192]{4,3,2,1,0:T(8,128)(2,1)S(1)}, u32[]{:S(2)}, u32[]{:S(2)}) collective-permute-start(bf16[1,2,3,12,192]{4,3,2,1,0:T(8,128)(2,1)S(1)} %slice.103), channel_id=1, source_target_pairs={{0,2},{2,4},{4,6},{6,0},{1,3},{3,5},{5,7},{7,1},{8,10},{10,12},{12... | collective-permute-start | bytes 82952 | tf_op jit(solution)/shard_map/ppermute | solution.py:24
  157.1 27.9 %collective-permute-start.5 = (bf16[1,2,6,6,192]{4,3,2,1,0:T(8,128)(2,1)S(1)}, bf16[1,2,6,6,192]{4,3,2,1,0:T(8,128)(2,1)S(1)}, u32[]{:S(2)}, u32[]{:S(2)}) collective-permute-start(bf16[1,2,6,6,192]{4,3,2,1,0:T(8,128)(2,1)S(1)} %fusion.15), channel_id=1, source_target_pairs={{0,8},{8,16},{16,24},{24,0},{1,9},{9,17},{17,25},{25,1},{2,10},{10... | collective-permute-start | bytes 82952 | tf_op jit(solution)/shard_map/ppermute | solution.py:24
Sparse Core Ops, SparseCore 0:
  88.0 41.3 all-reduce.9
  132.5 50.9 all-reduce.7
  186.3 10.7 reduce-scatter.4
  199.9 12.0 reduce-scatter.2
